TPU v7x, 32 devices: a whole 2x2x4 slice. The times are simulated.
32 devices in a mesh: dp: 16 (over z, y, core), tensor: 2 (over x).
Axes of the slice: x: 2, y: 2, z: 4, core: 2. Of those that a mesh axis runs over, the one named last changes fastest.
Arguments:
- hidden_in: bfloat16 [16384, 1024], P(('dp', 'tensor')), may hold values from -6 to 6
- w_z: bfloat16 [2, 1024, 2048], P(None, 'dp', 'tensor'), may hold values from -0.1875 to 0.1875
- w_x: bfloat16 [2, 1024, 2048], P(None, 'dp', 'tensor'), may hold values from -0.1875 to 0.1875
- w_dt: bfloat16 [2, 1024, 32], P(None, 'dp', 'tensor'), may hold values from -0.1875 to 0.1875
- w_bc: bfloat16 [2, 1024, 256], P(None, ('dp', 'tensor')), may hold values from -0.1875 to 0.1875
- w_out: bfloat16 [2, 2048, 1024], P(None, 'tensor', 'dp'), may hold values from -0.125 to 0.125
- conv_x: float32 [2, 4, 2048], P(None, None, 'tensor'), may hold values from -3 to 3
- conv_bc: float32 [2, 4, 256], replicated, may hold values from -3 to 3
- bias_x: float32 [2, 2048], P(None, 'tensor'), may hold values from -0.5 to 0.5
- bias_bc: float32 [2, 256], replicated, may hold values from -0.5 to 0.5
- dt_bias: float32 [2, 32], P(None, 'tensor'), may hold values from -4 to -1
- a_log: float32 [2, 32], P(None, 'tensor'), may hold values from -3 to 1.5
- d_skip: float32 [2, 32], P(None, 'tensor'), may hold values from 0.5 to 1.5
- gate_gain: float32 [2, 2048], P(None, 'tensor'), may hold values from 0.5 to 1.5
- pre_gain: float32 [2, 1024], replicated, may hold values from 0.5 to 1.5
- seq_lengths: int32 [16, 4], P('dp'), may hold values from 0 to 1024, as said below
- cotangent: bfloat16 [16384, 1024], P(('dp', 'tensor')), may hold values from -6 to 6
Outputs:
- hidden_out: bfloat16 [16384, 1024], P(('dp', 'tensor'))
- grad_hidden: float32 [16384, 1024], P(('dp', 'tensor'))
- grad_w_z: float32 [2, 1024, 2048], P(None, 'dp', 'tensor')
- grad_w_x: float32 [2, 1024, 2048], P(None, 'dp', 'tensor')
- grad_w_dt: float32 [2, 1024, 32], P(None, 'dp', 'tensor')
- grad_w_bc: float32 [2, 1024, 256], P(None, ('dp', 'tensor'))
- grad_w_out: float32 [2, 2048, 1024], P(None, 'tensor', 'dp')
- grad_conv_x: float32 [2, 4, 2048], P(None, None, 'tensor')
- grad_conv_bc: float32 [2, 4, 256], replicated
- grad_bias_x: float32 [2, 2048], P(None, 'tensor')
- grad_bias_bc: float32 [2, 256], replicated
- grad_dt_bias: float32 [2, 32], P(None, 'tensor')
- grad_a_log: float32 [2, 32], P(None, 'tensor')
- grad_d_skip: float32 [2, 32], P(None, 'tensor')
- grad_gate_gain: float32 [2, 2048], P(None, 'tensor')
- grad_pre_gain: float32 [2, 1024], replicated
Inputs may be any that keep to these rules, and one draw needn't show every extreme that they name: `seq_lengths`: row g lists the lengths of the sequences packed, in slot order from the first slot, into dp group g's 1024 token slots; a row sums to at most 1024 and the slots after its sum are padding; a length may be 0; in every draw some row is a single sequence of 1024 tokens.
All inputs are finite; a program needn't handle non-finite values.
Results may differ from a plain program's by a relative error of at most 0.024.
Values may be sent and summed in bfloat16 or wider, within the bound.
A program may use at most 320 MiB of HBM per device.

v0:
```python
from functools import partial

import jax
import jax.numpy as jnp
from jax import lax
from jax.sharding import PartitionSpec as P

INNER = 2048
SPAN = 256
LAYERS = 2
SLOTS = 4


epsilon = 1e-05
highest = lax.Precision.HIGHEST


def segment_ids(lengths, count):
    ends = jnp.cumsum(lengths)
    places = jnp.arange(count, dtype=jnp.int32)
    return jnp.sum((places[:, None] >= ends[None, :]).astype(jnp.int32), axis=1)


def causal_conv(values, kernel, offset, seg_ids):
    total = offset[None, :] + kernel[-1][None, :] * values
    for back_step in range(1, kernel.shape[0]):
        moved = jnp.concatenate(
            [jnp.zeros((back_step, values.shape[1]), jnp.float32), values[:-back_step]], axis=0
        )
        moved_ids = jnp.concatenate([jnp.full((back_step,), -1, jnp.int32), seg_ids[:-back_step]])
        same_seq = (moved_ids == seg_ids).astype(jnp.float32)
        total = total + kernel[-1 - back_step][None, :] * moved * same_seq[:, None]
    return total


def state_scan(channels, step_sizes, decay_rate, b_mat, c_mat, seg_ids, block_len):
    count, nheads = step_sizes.shape
    head_width = channels.shape[1] // nheads
    nstate = b_mat.shape[1]
    nblocks = count // block_len
    xs = channels.reshape(nblocks, block_len, nheads, head_width)
    steps_h = jnp.transpose(step_sizes.reshape(nblocks, block_len, nheads), (0, 2, 1))
    bs = b_mat.reshape(nblocks, block_len, nstate)
    cs = c_mat.reshape(nblocks, block_len, nstate)
    ids = seg_ids.reshape(nblocks, block_len)
    cumul = jnp.cumsum(steps_h * decay_rate[None, :, None], axis=2)
    scores = jnp.einsum("cin,cjn->cij", cs, bs, precision=highest)
    places = jnp.arange(block_len)
    allowed = (ids[:, :, None] == ids[:, None, :]) & (places[:, None] >= places[None, :])[None]
    spread = cumul[:, :, :, None] - cumul[:, :, None, :]
    decay = jnp.exp(jnp.where(allowed[:, None, :, :], spread, -1e30))
    mixing = scores[:, None, :, :] * decay * steps_h[:, :, None, :]
    inside = jnp.einsum("chij,cjhp->cihp", mixing, xs, precision=highest)
    last_ids = ids[:, -1]
    tail = (
        jnp.exp(jnp.where((ids == last_ids[:, None])[:, None, :], cumul[:, :, -1:] - cumul, -1e30))
        * steps_h
    )
    fresh = jnp.einsum("chj,cjn,cjhp->chpn", tail, bs, xs, precision=highest)
    prev_ids = jnp.concatenate([jnp.full((1,), -1, jnp.int32), last_ids[:-1]])
    keep_flag = (last_ids == prev_ids).astype(jnp.float32)
    carry_decay = jnp.exp(cumul[:, :, -1]) * keep_flag[:, None]

    def advance(state, inputs):
        factor, newer = inputs
        return (factor[:, None, None] * state + newer, state)

    _, before = lax.scan(
        advance, jnp.zeros((nheads, head_width, nstate), jnp.float32), (carry_decay, fresh)
    )
    reach = jnp.exp(cumul) * (ids == prev_ids[:, None]).astype(jnp.float32)[:, None, :]
    outside = (
        jnp.einsum("cin,chpn->cihp", cs, before, precision=highest)
        * jnp.transpose(reach, (0, 2, 1))[..., None]
    )
    return (inside + outside).reshape(count, nheads * head_width)


def mixer_core(
    proj_x,
    proj_bc,
    proj_dt,
    conv_x,
    bias_x,
    conv_bc,
    bias_bc,
    dt_bias,
    a_log,
    d_skip,
    seg_ids,
    block_len,
):
    x_conv = jax.nn.silu(causal_conv(proj_x, conv_x, bias_x, seg_ids))
    bc_conv = jax.nn.silu(causal_conv(proj_bc, conv_bc, bias_bc, seg_ids))
    nstate = bc_conv.shape[1] // 2
    step_sizes = jax.nn.softplus(proj_dt + dt_bias[None, :])
    head_width = x_conv.shape[1] // step_sizes.shape[1]
    scanned = state_scan(
        x_conv,
        step_sizes,
        -jnp.exp(a_log),
        bc_conv[:, :nstate],
        bc_conv[:, nstate:],
        seg_ids,
        block_len,
    )
    return scanned + jnp.repeat(d_skip, head_width)[None, :] * x_conv


def fetch_weights(w_z, w_x, w_dt, w_bc, w_out, layer_index):
    owned = (
        lax.all_gather(w_z[layer_index], "dp", axis=0, tiled=True),
        lax.all_gather(w_x[layer_index], "dp", axis=0, tiled=True),
        lax.all_gather(w_dt[layer_index], "dp", axis=0, tiled=True),
        lax.all_gather(w_out[layer_index], "dp", axis=1, tiled=True),
    )
    shared = lax.all_gather(w_bc[layer_index], ("dp", "tensor"), axis=0, tiled=True)
    return (owned[0], owned[1], owned[2], shared, owned[3])


def fetch_again(w_z, w_x, w_dt, w_bc, w_out, layer_index):
    owned = (
        lax.all_gather(w_z[layer_index], "dp", axis=0, tiled=True),
        lax.all_gather(w_x[layer_index], "dp", axis=0, tiled=True),
        lax.all_gather(w_dt[layer_index], "dp", axis=0, tiled=True),
        lax.all_gather(w_out[layer_index], "dp", axis=1, tiled=True),
    )
    shared = lax.all_gather(w_bc[layer_index], ("dp", "tensor"), axis=0, tiled=True)
    return (owned[0], owned[1], owned[2], shared, owned[3])


def per_device(
    hidden_in,
    w_z,
    w_x,
    w_dt,
    w_bc,
    w_out,
    conv_x,
    conv_bc,
    bias_x,
    bias_bc,
    dt_bias,
    a_log,
    d_skip,
    gate_gain,
    pre_gain,
    seq_lengths,
    cotangent,
):
    tok_rows = hidden_in.shape[0]
    group_rows = tok_rows * lax.axis_size("tensor")
    seg_ids = segment_ids(seq_lengths[0], group_rows)
    live_all = (seg_ids < SLOTS).astype(jnp.float32)
    live_rows = lax.dynamic_slice_in_dim(live_all, lax.axis_index("tensor") * tok_rows, tok_rows, 0)
    inner_part = w_z.shape[2]
    head_part = w_dt.shape[2]
    stream = hidden_in.astype(jnp.float32)
    stored = []
    for layer_index in range(LAYERS):
        weight_set = fetch_weights(w_z, w_x, w_dt, w_bc, w_out, layer_index)
        scale_pre = lax.rsqrt(jnp.mean(stream * stream, axis=1) + epsilon)
        normed = (stream * scale_pre[:, None] * pre_gain[layer_index][None, :]).astype(jnp.bfloat16)
        normed_all = lax.all_gather(normed, "tensor", axis=0, tiled=True)
        joined = jnp.concatenate(weight_set[:4], axis=1)
        projected = jnp.dot(normed_all, joined, preferred_element_type=jnp.float32)
        gate_raw = projected[:, :inner_part]
        proj_x = projected[:, inner_part : 2 * inner_part]
        proj_dt = projected[:, 2 * inner_part : 2 * inner_part + head_part]
        proj_bc = projected[:, 2 * inner_part + head_part :]
        mixed, back_fn = jax.vjp(
            partial(mixer_core, seg_ids=seg_ids, block_len=SPAN),
            proj_x,
            proj_bc,
            proj_dt,
            conv_x[layer_index],
            bias_x[layer_index],
            conv_bc[layer_index],
            bias_bc[layer_index],
            dt_bias[layer_index],
            a_log[layer_index],
            d_skip[layer_index],
        )
        gated = mixed * jax.nn.silu(gate_raw)
        square_sum = lax.psum(jnp.sum(gated * gated, axis=1), "tensor")
        scale_gate = lax.rsqrt(square_sum / INNER + epsilon)
        normed_out = (gated * scale_gate[:, None] * gate_gain[layer_index][None, :]).astype(
            jnp.bfloat16
        )
        out_matrix = weight_set[4]
        branch = (
            lax.psum_scatter(
                jnp.dot(normed_out, out_matrix, preferred_element_type=jnp.float32).astype(
                    jnp.bfloat16
                ),
                "tensor",
                scatter_dimension=0,
                tiled=True,
            ).astype(jnp.float32)
            * live_rows[:, None]
        )
        stored.append(
            (
                stream,
                scale_pre,
                normed_all,
                gate_raw,
                mixed,
                gated,
                scale_gate,
                normed_out,
                back_fn,
                weight_set,
            )
        )
        stream = stream + branch
    hidden_out = stream.astype(jnp.bfloat16)
    grads = [[None] * LAYERS for name_index in range(14)]
    stream_grad = cotangent.astype(jnp.float32)
    for layer_index in reversed(range(LAYERS)):
        (
            stream_in,
            scale_pre,
            normed_all,
            gate_raw,
            mixed,
            gated,
            scale_gate,
            normed_out,
            back_fn,
            weight_set,
        ) = stored[layer_index]
        used_set = fetch_again(w_z, w_x, w_dt, w_bc, w_out, layer_index)
        joined = jnp.concatenate(used_set[:4], axis=1)
        branch_grad = (stream_grad * live_rows[:, None]).astype(jnp.bfloat16)
        grad_all = lax.all_gather(branch_grad, "tensor", axis=0, tiled=True)
        grad_out = jnp.einsum("gi,gd->id", normed_out, grad_all, preferred_element_type=jnp.float32)
        d_normed_out = jnp.einsum(
            "gd,id->gi", grad_all, used_set[4], preferred_element_type=jnp.float32
        )
        gain_row = gate_gain[layer_index]
        grad_gain = jnp.sum(d_normed_out * gated * scale_gate[:, None], axis=0)
        inner_dot = lax.psum(jnp.sum(d_normed_out * gain_row[None, :] * gated, axis=1), "tensor")
        d_gated = (
            scale_gate[:, None] * gain_row[None, :] * d_normed_out
            - gated * (scale_gate**3 * inner_dot / INNER)[:, None]
        )
        sigmoid_gate = jax.nn.sigmoid(gate_raw)
        d_mixed = d_gated * gate_raw * sigmoid_gate
        d_gate_raw = d_gated * mixed * sigmoid_gate * (1.0 + gate_raw * (1.0 - sigmoid_gate))
        pieces = back_fn(d_mixed)
        d_proj = jnp.concatenate([d_gate_raw, pieces[0], pieces[2], pieces[1]], axis=1).astype(
            jnp.bfloat16
        )
        grad_joined = jnp.einsum(
            "gd,gk->dk", normed_all, d_proj, preferred_element_type=jnp.float32
        )
        grad_wz = grad_joined[:, :inner_part]
        grad_wx = grad_joined[:, inner_part : 2 * inner_part]
        grad_wdt = grad_joined[:, 2 * inner_part : 2 * inner_part + head_part]
        grad_wbc = grad_joined[:, 2 * inner_part + head_part :]
        owned_grads = (
            lax.psum_scatter(
                grad_wz.astype(jnp.bfloat16), "dp", scatter_dimension=0, tiled=True
            ).astype(jnp.float32),
            lax.psum_scatter(
                grad_wx.astype(jnp.bfloat16), "dp", scatter_dimension=0, tiled=True
            ).astype(jnp.float32),
            lax.psum_scatter(
                grad_wdt.astype(jnp.bfloat16), "dp", scatter_dimension=0, tiled=True
            ).astype(jnp.float32),
            lax.psum_scatter(
                grad_out.astype(jnp.bfloat16), "dp", scatter_dimension=1, tiled=True
            ).astype(jnp.float32),
        )
        grads[3][layer_index] = lax.psum_scatter(
            grad_wbc, ("dp", "tensor"), scatter_dimension=0, tiled=True
        )
        grads[0][layer_index] = owned_grads[0]
        grads[1][layer_index] = owned_grads[1]
        grads[2][layer_index] = owned_grads[2]
        grads[4][layer_index] = owned_grads[3]
        d_normed = lax.psum_scatter(
            jnp.einsum("gk,dk->gd", d_proj, joined, preferred_element_type=jnp.float32).astype(
                jnp.bfloat16
            ),
            "tensor",
            scatter_dimension=0,
            tiled=True,
        ).astype(jnp.float32)
        pre_row = pre_gain[layer_index]
        grad_pre = jnp.sum(d_normed * stream_in * scale_pre[:, None], axis=0)
        pre_dot = jnp.mean(d_normed * pre_row[None, :] * stream_in, axis=1)
        stream_grad = (
            stream_grad
            + scale_pre[:, None] * pre_row[None, :] * d_normed
            - stream_in * (scale_pre**3 * pre_dot)[:, None]
        )
        head_sums = lax.psum(
            (pieces[3], pieces[4], pieces[7], pieces[8], pieces[9], grad_gain), "dp"
        )
        shared_sums = lax.psum((pieces[5], pieces[6], grad_pre), ("dp", "tensor"))
        grads[5][layer_index] = head_sums[0]
        grads[7][layer_index] = head_sums[1]
        grads[9][layer_index] = head_sums[2]
        grads[10][layer_index] = head_sums[3]
        grads[11][layer_index] = head_sums[4]
        grads[12][layer_index] = head_sums[5]
        grads[6][layer_index] = shared_sums[0]
        grads[8][layer_index] = shared_sums[1]
        grads[13][layer_index] = shared_sums[2]
    stacked = [jnp.stack(entry, axis=0) for entry in grads]
    return (
        hidden_out,
        stream_grad,
        stacked[0],
        stacked[1],
        stacked[2],
        stacked[3],
        stacked[4],
        stacked[5],
        stacked[6],
        stacked[7],
        stacked[8],
        stacked[9],
        stacked[10],
        stacked[11],
        stacked[12],
        stacked[13],
    )


def solution(mesh):
    return jax.shard_map(
        per_device,
        mesh=mesh,
        in_specs=(
            P(("dp", "tensor"), None),
            P(None, "dp", "tensor"),
            P(None, "dp", "tensor"),
            P(None, "dp", "tensor"),
            P(None, ("dp", "tensor"), None),
            P(None, "tensor", "dp"),
            P(None, None, "tensor"),
            P(),
            P(None, "tensor"),
            P(),
            P(None, "tensor"),
            P(None, "tensor"),
            P(None, "tensor"),
            P(None, "tensor"),
            P(),
            P("dp", None),
            P(("dp", "tensor"), None),
        ),
        out_specs=(
            P(("dp", "tensor"), None),
            P(("dp", "tensor"), None),
            P(None, "dp", "tensor"),
            P(None, "dp", "tensor"),
            P(None, "dp", "tensor"),
            P(None, ("dp", "tensor"), None),
            P(None, "tensor", "dp"),
            P(None, None, "tensor"),
            P(),
            P(None, "tensor"),
            P(),
            P(None, "tensor"),
            P(None, "tensor"),
            P(None, "tensor"),
            P(None, "tensor"),
            P(),
        ),
        check_vma=False,
    )
```

profile of v0, /device:TPU:0, one launch (start us, length us, event | category | flops | bytes accessed | tf_op | source)
XLA Modules:
  0.0 1647.5 jit_solution(2040046657451041489)
XLA Ops:
  21.7 25.3 %all-gather.2 = bf16[1,1024,16]{2,0,1:T(2,128)(2,1)S(1)} all-gather(bf16[1,64,16]{2,0,1:T(2,128)(2,1)S(1)} %copy.518), channel_id=4, replica_groups=mesh['dp'=16,'tensor'=2] {'dp'}, dimensions={1}, use_global_device_ids=true | all-gather | bytes 34816 | tf_op jit(solution)/shard_map/all_gather | solution.py:114
  47.0 69.5 %all-gather.3 = bf16[1,1024,256]{2,1,0:T(8,128)(2,1)S(1)} all-gather(bf16[1,32,256]{2,1,0:T(8,128)(2,1)S(1)} %get-tuple-element.761), channel_id=5, replica_groups=mesh['dp'=16,'tensor'=2] {'dp','tensor'}, dimensions={1}, use_global_device_ids=true | all-gather | bytes 540672 | tf_op jit(solution)/shard_map/all_gather | solution.py:117
  117.5 8.2 concatenate.81
  125.7 7.8 all-gather.21.cloned.1.call-done
  133.4 8.2 fusion.244
  159.4 10.6 fusion.57
  176.7 7.6 fusion.72
  205.4 19.8 %bitcast_add_fusion.7 = f32[4,256,16,64]{1,3,2,0:T(8,128)S(1)} fusion(f32[4,256,16,64]{1,3,2,0:T(8,128)S(1)} %fusion.246, f32[4,256,16]{1,2,0:T(8,128)S(1)} %get-tuple-element.750, f32[4,16,256]{2,1,0:T(8,128)S(1)} %bitcast.617, f32[4,16,256]{2,1,0:T(8,128)S(1)} %copy_bitcast_fusion.3, f32[4,256,256]{2,1,0:T(8,128)S(1)} %fusion.245, ...), kind=kOutput, calls=%fused_computation.95 | convolution fusion | flops 3240099840 | bytes 14090240 | tf_op jit(solution)/shard_map/jvp(chij,cjhp->cihp)/dot_general | solution.py:53
  249.9 30.7 %reduce-scatter.31.cloned.1.call-done = bf16[512,1024]{1,0:T(8,128)(2,1)} async-done(((bf16[1024,1024]{1,0:T(8,128)(2,1)}), bf16[512,1024]{1,0:T(8,128)(2,1)}) %reduce-scatter.31.cloned.1.call-update) | async-done | bytes 1048592 | tf_op jit(solution)/shard_map/reduce_scatter | solution.py:192
  286.6 23.6 %all-gather.7 = bf16[1,1024,16]{2,0,1:T(2,128)(2,1)S(1)} all-gather(bf16[1,64,16]{2,0,1:T(2,128)(2,1)S(1)} %copy.519), channel_id=9, replica_groups=mesh['dp'=16,'tensor'=2] {'dp'}, dimensions={1}, use_global_device_ids=true | all-gather | bytes 34816 | tf_op jit(solution)/shard_map/all_gather | solution.py:114
  310.2 68.2 %all-gather.8 = bf16[1,1024,256]{2,1,0:T(8,128)(2,1)S(1)} all-gather(bf16[1,32,256]{2,1,0:T(8,128)(2,1)S(1)} %get-tuple-element.760), channel_id=10, replica_groups=mesh['dp'=16,'tensor'=2] {'dp','tensor'}, dimensions={1}, use_global_device_ids=true | all-gather | bytes 540672 | tf_op jit(solution)/shard_map/all_gather | solution.py:117
  378.5 8.2 concatenate.93
  386.7 16.0 all-gather.23.cloned.1.call-done
  402.7 8.2 fusion.247
  442.2 10.3 fusion.56
  458.3 7.6 fusion.68
  480.9 19.5 %bitcast_add_fusion.6 = f32[4,256,16,64]{1,3,2,0:T(8,128)S(1)} fusion(f32[4,256,16,64]{1,3,2,0:T(8,128)S(1)} %fusion.249, f32[4,256,16]{1,2,0:T(8,128)S(1)} %get-tuple-element.748, f32[4,16,256]{2,1,0:T(8,128)S(1)} %bitcast.620, f32[4,16,256]{2,1,0:T(8,128)S(1)} %copy_bitcast_fusion.2, f32[4,256,256]{2,1,0:T(8,128)S(1)} %fusion.248, ...), kind=kOutput, calls=%fused_computation.94 | convolution fusion | flops 3240099840 | bytes 14090240 | tf_op jit(solution)/shard_map/jvp(chij,cjhp->cihp)/dot_general | solution.py:53
  516.6 9.0 multiply_reduce_fusion.6
  530.5 11.6 multiply_reduce_fusion.8
  559.5 27.6 %fusion.19 = (f32[4,16,256]{2,1,0:T(8,128)}, f32[4,16,256]{2,1,0:T(8,128)}, f32[4,16,256]{2,1,0:T(8,128)}, f32[4,256,256]{2,1,0:T(8,128)S(1)}) fusion(f32[4,16,256]{2,1,0:T(8,128)S(1)} %bitcast.621, f32[4,16,256]{2,1,0:T(8,128)S(1)} %copy_bitcast_fusion.2, f32[4,256,256]{2,1,0:T(8,128)S(1)} %copy-done.93, pred[4,256,256]{2,1,0:T(8,128)(4,1)S(1)} %copy-done.102, ...), kind=kOutput, calls=%fused_computation.39 | convolution fusion | flops 3275440128 | bytes 11075584 | tf_op jit(solution)/shard_map/transpose(jvp(chij,cjhp->cihp))/dot_general | solution.py:53
  598.0 11.2 while.70
  610.8 9.6 fusion.145
  626.6 15.2 bitcast_add_fusion.5
  662.1 8.3 multiply_reduce_fusion.12
  671.6 9.9 reduce-window.44
  702.0 10.2 convolution_convert_fusion.3
  712.3 31.9 %reduce-scatter.35.cloned.1.call-done = bf16[512,1024]{1,0:T(8,128)(2,1)} async-done(((bf16[1024,1024]{1,0:T(8,128)(2,1)}), bf16[512,1024]{1,0:T(8,128)(2,1)}) %reduce-scatter.35.cloned.1.call-update) | async-done | bytes 1048592 | tf_op jit(solution)/shard_map/reduce_scatter | solution.py:283
  750.4 11.7 fusion.242
  783.7 9.1 multiply_reduce_fusion.7
  797.6 11.7 multiply_reduce_fusion.9
  827.2 27.5 %fusion.21 = (f32[4,16,256]{2,1,0:T(8,128)}, f32[4,16,256]{2,1,0:T(8,128)}, f32[4,16,256]{2,1,0:T(8,128)}, f32[4,256,256]{2,1,0:T(8,128)S(1)}) fusion(f32[4,16,256]{2,1,0:T(8,128)S(1)} %bitcast.618, f32[4,16,256]{2,1,0:T(8,128)S(1)} %copy-done.109, f32[4,256,256]{2,1,0:T(8,128)S(1)} %copy-done.90, pred[4,256,256]{2,1,0:T(8,128)(4,1)S(1)} %copy-done.104, ...), kind=kOutput, calls=%fused_computation.41 | convolution fusion | flops 3275440128 | bytes 11075584 | tf_op jit(solution)/shard_map/transpose(jvp(chij,cjhp->cihp))/dot_general | solution.py:53
  863.8 11.2 while.71
  876.0 10.0 fusion.142
  892.1 15.1 bitcast_add_fusion.4
  927.7 8.2 multiply_reduce_fusion.16
  937.0 9.9 reduce-window.55
  965.3 13.8 fusion.243
  1010.0 9.7 convolution_convert_fusion.2
  1028.9 13.8 reduce-scatter.49.cloned.1.call-done
  1043.7 63.3 %reduce-scatter.45.cloned.1.call-done = bf16[64,1024]{1,0:T(8,128)(2,1)} async-done(((bf16[1024,1024]{1,0:T(8,128)(2,1)}), bf16[64,1024]{1,0:T(8,128)(2,1)}) %reduce-scatter.45.cloned.1.call-update) | async-done | bytes 131088
  1108.4 57.8 %all-reduce.51 = (f32[1,4,1024]{2,1,0:T(4,128)S(1)}, f32[1,4,1024]{2,1,0:T(4,128)S(1)}, f32[1,1024]{1,0:T(1,128)S(1)}, f32[1,1024]{1,0:T(1,128)S(1)}, f32[1,16]{...) all-reduce(f32[1,4,1024]{2,1,0:T(4,128)S(1)} %add_bitcast_fusion.4,, ...), channel_id=1, replica_groups=mesh['dp'=16,'tensor'=2] {'dp'}, use_global_device_ids=true, to_apply=%region_67.69 | all-reduce | flops 12384 | bytes 99072 | tf_op jit(solution)/shard_map/psum | solution.py:299
  1170.1 133.8 %reduce-scatter.55.cloned.1.call-done = f32[32,256]{1,0:T(8,128)} async-done(((f32[1024,256]{1,0:T(8,128)}), f32[32,256]{1,0:T(8,128)}) %reduce-scatter.55.cloned.1.call-update) | async-done | bytes 32784
  1305.5 59.9 %reduce-scatter.47.cloned.1.call-done = bf16[64,1024]{1,0:T(8,128)(2,1)} async-done(((bf16[1024,1024]{1,0:T(8,128)(2,1)}), bf16[64,1024]{1,0:T(8,128)(2,1)}) %reduce-scatter.47.cloned.1.call-update) | async-done | bytes 131088
  1370.2 59.6 %reduce-scatter.43.cloned.1.call-done = bf16[64,1024]{1,0:T(8,128)(2,1)} async-done(((bf16[1024,1024]{1,0:T(8,128)(2,1)}), bf16[64,1024]{1,0:T(8,128)(2,1)}) %reduce-scatter.43.cloned.1.call-update) | async-done | bytes 131088
  1435.9 58.4 %reduce-scatter.41.cloned.1.call-done = bf16[1024,64]{0,1:T(8,128)(2,1)} async-done(((bf16[1024,1024]{0,1:T(8,128)(2,1)}), bf16[1024,64]{0,1:T(8,128)(2,1)}) %reduce-scatter.41.cloned.1.call-update) | async-done | bytes 131088 | tf_op jit(solution)/shard_map/reduce_scatter | solution.py:272
  1494.3 64.5 %reduce-scatter.39.cloned.1.call-done = bf16[1024,64]{0,1:T(8,128)(2,1)} async-done(((bf16[1024,1024]{0,1:T(8,128)(2,1)}), bf16[1024,64]{0,1:T(8,128)(2,1)}) %reduce-scatter.39.cloned.1.call-update) | async-done | bytes 131088 | tf_op jit(solution)/shard_map/reduce_scatter | solution.py:272
  1560.6 31.4 %reduce-scatter.37.cloned.1.call-done = bf16[512,1024]{1,0:T(8,128)(2,1)} async-done(((bf16[1024,1024]{1,0:T(8,128)(2,1)}), bf16[512,1024]{1,0:T(8,128)(2,1)}) %reduce-scatter.37.cloned.1.call-update) | async-done | bytes 1048592 | tf_op jit(solution)/shard_map/reduce_scatter | solution.py:283
  1594.1 40.1 %all-reduce.50 = (f32[1,4,256]{2,1,0:T(4,128)S(1)}, f32[1,4,256]{2,1,0:T(4,128)S(1)}, f32[1,256]{1,0:T(1,128)S(1)}, f32[1,256]{1,0:T(1,128)S(1)}, f32[1,1024]{1,0:T(1,128)S(1)}, /*index=5*/f32[1,1024]{1,0:T(1,128)S(1)}) all-reduce(f32[1,4,256]{2,1,0:T(4,128)S(1)} %get-tuple-element.812, ...), channel_id=1, replica_groups=mesh['dp'=16,'tensor'=2] {'dp','tensor'}, use_global_device_ids=true, to_apply=%region_77.79 | all-reduce | flops 4608 | bytes 36864 | tf_op jit(solution)/shard_map/psum | solution.py:302
  (817 shorter events, 448.1 us)
Async XLA Ops:
  7.3 110.2 %all-gather.29.cloned.1.call-start = ((), (), s32[]{:S(2)}) async-start(), calls=%async_computation.24 | async-start | bytes 2228224 | tf_op jit(solution)/shard_map/all_gather | solution.py:112
  9.1 108.3 %all-gather.31.cloned.1.call-start = ((), (), s32[]{:S(2)}) async-start(), calls=%async_computation.25 | async-start | bytes 2228224 | tf_op jit(solution)/shard_map/all_gather | solution.py:113
  10.9 122.6 %all-gather.21.cloned.1.call-start = ((), (), s32[]{:S(2)}) async-start(), calls=%async_computation.14 | async-start | bytes 3145728 | tf_op jit(solution)/shard_map/all_gather | solution.py:164
  13.3 269.1 %copy-start.113 = (f32[1,1024]{1,0:T(1,128)}, f32[1,1024]{1,0:T(1,128)S(1)}, u32[]{:S(2)}) copy-start(f32[1,1024]{1,0:T(1,128)S(1)} %get-tuple-element.777) | copy-start | bytes 12292
  15.8 225.6 %all-gather.33.cloned.1.call-start = ((), (), s32[]{:S(2)}) async-start(), calls=%async_computation.26 | async-start | bytes 2228224 | tf_op jit(solution)/shard_map/all_gather | solution.py:115
  16.6 264.0 %reduce-scatter.31.cloned.1.call-start = ((), (), s32[]{:S(2)}) async-start(), calls=%async_computation.15 | async-start | bytes 3145728 | tf_op jit(solution)/shard_map/reduce_scatter | solution.py:192
  18.7 210.3 %copy-start.133 = (f32[1024]{0:T(1024)}, f32[1024]{0:T(1024)S(1)}, u32[]{:S(2)}) copy-start(f32[1024]{0:T(1024)S(1)} %mul.1316) | copy-start | bytes 12292
  19.9 221.5 %copy-start.174 = (f32[1,1024]{1,0:T(1,128)}, f32[1,1024]{1,0:T(1,128)S(1)}, u32[]{:S(2)}) copy-start(f32[1,1024]{1,0:T(1,128)S(1)} %get-tuple-element.763) | copy-start | bytes 12292
  20.7 421.5 %copy-start.148 = (f32[1,1,1024]{2,1,0:T(1,128)}, f32[1,1,1024]{2,1,0:T(1,128)S(1)}, u32[]{:S(2)}) copy-start(f32[1,1,1024]{2,1,0:T(1,128)S(1)} %get-tuple-element.752) | copy-start | bytes 12292
  20.7 421.5 %copy-start.150 = (f32[1,1,1024]{2,1,0:T(1,128)}, f32[1,1,1024]{2,1,0:T(1,128)S(1)}, u32[]{:S(2)}) copy-start(f32[1,1,1024]{2,1,0:T(1,128)S(1)} %get-tuple-element.758) | copy-start | bytes 12292
  20.7 421.5 %copy-start.152 = (f32[1,1,1024]{2,1,0:T(1,128)}, f32[1,1,1024]{2,1,0:T(1,128)S(1)}, u32[]{:S(2)}) copy-start(f32[1,1,1024]{2,1,0:T(1,128)S(1)} %get-tuple-element.753) | copy-start | bytes 12292
  117.4 302.9 %copy-start.111 = (f32[4,256]{1,0:T(4,128)}, f32[4,256]{1,0:T(4,128)S(1)}, u32[]{:S(2)}) copy-start(f32[4,256]{1,0:T(4,128)S(1)} %get-tuple-element.778) | copy-start | bytes 12292
  117.4 302.9 %copy-start.121 = (pred[4,256]{1,0:T(4,128)(4,1)}, pred[4,256]{1,0:T(4,128)(4,1)S(1)}, u32[]{:S(2)}) copy-start(pred[4,256]{1,0:T(4,128)(4,1)S(1)} %get-tuple-element.779) | copy-start | bytes 3076
  248.4 130.1 %all-gather.35.cloned.1.call-start = ((), (), s32[]{:S(2)}) async-start(), calls=%async_computation.27 | async-start | bytes 2228224 | tf_op jit(solution)/shard_map/all_gather | solution.py:112
  249.0 129.5 %all-gather.37.cloned.1.call-start = ((), (), s32[]{:S(2)}) async-start(), calls=%async_computation.28 | async-start | bytes 2228224 | tf_op jit(solution)/shard_map/all_gather | solution.py:113
  249.7 153.0 %all-gather.23.cloned.1.call-start = ((), (), s32[]{:S(2)}) async-start(), calls=%async_computation.16 | async-start | bytes 3145728 | tf_op jit(solution)/shard_map/all_gather | solution.py:164
  285.6 231.0 %all-gather.39.cloned.1.call-start = ((), (), s32[]{:S(2)}) async-start(), calls=%async_computation.29 | async-start | bytes 2228224 | tf_op jit(solution)/shard_map/all_gather | solution.py:115
  286.3 230.3 %all-gather.25.cloned.1.call-start = ((), (), s32[]{:S(2)}) async-start(), calls=%async_computation.18 | async-start | bytes 3145728 | tf_op jit(solution)/shard_map/all_gather | solution.py:236
  286.5 244.0 %copy-start.135 = (f32[1024]{0:T(1024)}, f32[1024]{0:T(1024)S(1)}, u32[]{:S(2)}) copy-start(f32[1024]{0:T(1024)S(1)} %mul.1380) | copy-start | bytes 12292
  386.7 357.5 %reduce-scatter.35.cloned.1.call-start = ((), (), s32[]{:S(2)}) async-start(), calls=%async_computation.19 | async-start | bytes 3145728 | tf_op jit(solution)/shard_map/reduce_scatter | solution.py:283
  712.2 71.4 %all-gather.27.cloned.1.call-start = ((), (), s32[]{:S(2)}) async-start(), calls=%async_computation.20 | async-start | bytes 3145728 | tf_op jit(solution)/shard_map/all_gather | solution.py:236
  750.4 276.7 %reduce-scatter.53.cloned.1.call-start = ((), (), s32[]{:S(2)}) async-start(), calls=%async_computation.35 | async-start | bytes 278528
  765.3 262.6 %reduce-scatter.57.cloned.1.call-start = ((), (), s32[]{:S(2)}) async-start(), calls=%async_computation.37 | async-start | bytes 1081344
  768.0 274.6 %reduce-scatter.49.cloned.1.call-start = ((), (), s32[]{:S(2)}) async-start(), calls=%async_computation.33 | async-start | bytes 2228224
  776.0 331.0 %reduce-scatter.45.cloned.1.call-start = ((), (), s32[]{:S(2)}) async-start(), calls=%async_computation.31 | async-start | bytes 2228224
  778.7 389.9 %reduce-scatter.51.cloned.1.call-start = ((), (), s32[]{:S(2)}) async-start(), calls=%async_computation.34 | async-start | bytes 278528
  982.2 321.7 %reduce-scatter.55.cloned.1.call-start = ((), (), s32[]{:S(2)}) async-start(), calls=%async_computation.36 | async-start | bytes 1081344
  984.9 380.6 %reduce-scatter.47.cloned.1.call-start = ((), (), s32[]{:S(2)}) async-start(), calls=%async_computation.32 | async-start | bytes 2228224
  993.0 436.8 %reduce-scatter.43.cloned.1.call-start = ((), (), s32[]{:S(2)}) async-start(), calls=%async_computation.30 | async-start | bytes 2228224
  995.7 498.6 %reduce-scatter.41.cloned.1.call-start = ((), (), s32[]{:S(2)}) async-start(), calls=%async_computation.23 | async-start | bytes 2228224 | tf_op jit(solution)/shard_map/reduce_scatter | solution.py:272
  1002.7 556.1 %reduce-scatter.39.cloned.1.call-start = ((), (), s32[]{:S(2)}) async-start(), calls=%async_computation.22 | async-start | bytes 2228224 | tf_op jit(solution)/shard_map/reduce_scatter | solution.py:272
  1009.9 582.1 %reduce-scatter.37.cloned.1.call-start = ((), (), s32[]{:S(2)}) async-start(), calls=%async_computation.21 | async-start | bytes 3145728 | tf_op jit(solution)/shard_map/reduce_scatter | solution.py:283
  1019.8 147.5 %copy-start.197 = (f32[256]{0:T(256)S(1)}, f32[256]{0:T(256)}, u32[]{:S(2)}) copy-start(f32[256]{0:T(256)} %get-tuple-element.669) | copy-start | bytes 3076
  1019.8 147.5 %copy-start.198 = (f32[256]{0:T(256)S(1)}, f32[256]{0:T(256)}, u32[]{:S(2)}) copy-start(f32[256]{0:T(256)} %get-tuple-element.672) | copy-start | bytes 3076
  1019.8 147.5 %copy-start.199 = (f32[256]{0:T(256)S(1)}, f32[256]{0:T(256)}, u32[]{:S(2)}) copy-start(f32[256]{0:T(256)} %get-tuple-element.732) | copy-start | bytes 3076
  1019.9 616.1 %reduce-scatter.33.cloned.1.call-start = ((), (), s32[]{:S(2)}) async-start(), calls=%async_computation.17 | async-start | bytes 3145728 | tf_op jit(solution)/shard_map/reduce_scatter | solution.py:192
  1168.6 423.3 %copy-start.19 = (bf16[512,1024]{1,0:T(8,128)(2,1)S(1)}, bf16[512,1024]{1,0:T(8,128)(2,1)}, u32[]{:S(2)}) copy-start(bf16[512,1024]{1,0:T(8,128)(2,1)} %param.26) | copy-start | bytes 3145732
  1168.6 423.3 %copy-start.128 = (f32[1,1024]{1,0:T(1,128)S(1)}, f32[1,1024]{1,0:T(1,128)}, u32[]{:S(2)}) copy-start(f32[1,1024]{1,0:T(1,128)} %copy-done.127) | copy-start | bytes 12292
  1168.6 423.3 %copy-start.159 = (f32[512]{0:T(512)S(1)}, f32[512]{0:T(512)}, u32[]{:S(2)}) copy-start(f32[512]{0:T(512)} %copy-done.158) | copy-start | bytes 6148
  1367.6 226.4 %copy-start.177 = (f32[1024]{0:T(1024)S(1)}, f32[1024]{0:T(1024)}, u32[]{:S(2)}) copy-start(f32[1024]{0:T(1024)} %get-tuple-element.584) | copy-start | bytes 12292
  1367.6 226.4 %copy-start.196 = (f32[256]{0:T(256)S(1)}, f32[256]{0:T(256)}, u32[]{:S(2)}) copy-start(f32[256]{0:T(256)} %get-tuple-element.590) | copy-start | bytes 3076
  1367.6 268.4 %copy-start.161 = (f32[512]{0:T(512)S(1)}, f32[512]{0:T(512)}, u32[]{:S(2)}) copy-start(f32[512]{0:T(512)} %copy-done.160) | copy-start | bytes 6148
  1367.6 268.4 %copy-start.35 = (bf16[512,1024]{1,0:T(8,128)(2,1)S(1)}, bf16[512,1024]{1,0:T(8,128)(2,1)}, u32[]{:S(2)}) copy-start(bf16[512,1024]{1,0:T(8,128)(2,1)} %reduce-scatter.31.cloned.1.call-done) | copy-start | bytes 3145732
  1367.6 268.4 %copy-start.57 = (bf16[512,1024]{1,0:T(8,128)(2,1)S(1)}, bf16[512,1024]{1,0:T(8,128)(2,1)}, u32[]{:S(2)}) copy-start(bf16[512,1024]{1,0:T(8,128)(2,1)} %param.42) | copy-start | bytes 3145732
  1367.7 268.4 %copy-start.115 = (f32[1,1024]{1,0:T(1,128)S(1)}, f32[1,1024]{1,0:T(1,128)}, u32[]{:S(2)}) copy-start(f32[1,1024]{1,0:T(1,128)} %copy-done.113) | copy-start | bytes 12292
  1367.7 268.4 %copy-start.126 = (f32[512]{0:T(512)S(1)}, f32[512]{0:T(512)}, u32[]{:S(2)}) copy-start(f32[512]{0:T(512)} %copy-done.124) | copy-start | bytes 6148
  1367.7 268.4 %copy-start.139 = (f32[512]{0:T(512)S(1)}, f32[512]{0:T(512)}, u32[]{:S(2)}) copy-start(f32[512]{0:T(512)} %copy-done.137) | copy-start | bytes 6148
  1367.7 268.4 %copy-start.165 = (f32[512]{0:T(512)S(1)}, f32[512]{0:T(512)}, u32[]{:S(2)}) copy-start(f32[512]{0:T(512)} %copy-done.164) | copy-start | bytes 6148
  (196 other events, 4710.3 us)
Sparse Core Ops, SparseCore 0:
  10.8 44.9 all-gather.28
  58.6 40.3 all-gather.30
  101.1 32.2 all-gather.20
  135.5 41.4 all-gather.32
  248.5 32.0 reduce-scatter.30
  283.2 42.9 all-gather.34
  328.3 40.1 all-gather.36
  370.7 31.9 all-gather.22
  404.9 41.4 all-gather.38
  447.8 31.7 all-gather.24
  712.3 31.8 reduce-scatter.34
  750.5 33.0 all-gather.26
  787.7 55.7 reduce-scatter.52
  845.6 135.6 reduce-scatter.56
  984.9 57.6 reduce-scatter.48
  1046.2 60.6 reduce-scatter.44
  1110.9 54.6 reduce-scatter.50
  1168.3 135.5 reduce-scatter.54
  1307.7 57.7 reduce-scatter.46
  1369.0 60.7 reduce-scatter.42
  1433.5 60.7 reduce-scatter.40
  1498.0 60.7 reduce-scatter.38
  1561.1 30.8 reduce-scatter.36
  1594.6 32.3 reduce-scatter.32
where the time goes:
time: 1660 us; the launch traced here: 1650 us
  waiting for transfers between devices  578 us (35%)
  matrix products  320 us (19%)
  blocking collectives  304 us (18%)
  other arithmetic  241 us (15%)
  local copies, waits for them, and re-layouts  185 us (11%)
  between operations  17.7 us (1%)
    unnamed x32, waiting for transfers between devices  333 us
    all_gather x2, blocking collectives, fetch_weights(): lax.all_gather(w_bc[layer_index], ('dp', 'tensor'), axis=0, tiled=True)  138 us
    dot_general x6, matrix products, state_scan(): inside = jnp.einsum('chij,cjhp->cihp', mixing, xs, precision=highest)  125 us
    reduce_scatter x2, waiting for transfers between devices, per_device(): lax.psum_scatter(grad_out.astype(jnp.bfloat16), 'dp', scatter_dimension=1...  123 us
    reduce_scatter x2, waiting for transfers between devices, per_device(): lax.psum_scatter(jnp.einsum('gk,dk->gd', d_proj, joined, preferred_elemen...  63.3 us
    unnamed x464, local copies, waits for them, and re-layouts  61.1 us
    psum x1, blocking collectives, per_device(): lax.psum((pieces[3], pieces[4], pieces[7], pieces[8], pieces[9], grad_gai...  57.8 us
    all_gather x2, blocking collectives, fetch_weights(): lax.all_gather(w_dt[layer_index], 'dp', axis=0, tiled=True)  48.8 us
  transfers between devices with their start and end apart: 24, of which 13 were waited for; matrix products, arithmetic and copies ran while one was open for 31% of the time, Pallas kernels for 0%

commit v1 on v0

--- a/solution.py
+++ b/solution.py
@@ -6,13 +6,13 @@
 from jax.sharding import PartitionSpec as P
 
 INNER = 2048
-SPAN = 256
+SPAN = 128
 LAYERS = 2
 SLOTS = 4
 
 
 epsilon = 1e-05
-highest = lax.Precision.HIGHEST
+highest = lax.Precision.HIGH
 
 
 def segment_ids(lengths, count):
@@ -66,7 +66,7 @@
         return (factor[:, None, None] * state + newer, state)
 
     _, before = lax.scan(
-        advance, jnp.zeros((nheads, head_width, nstate), jnp.float32), (carry_decay, fresh)
+        advance, jnp.zeros((nheads, head_width, nstate), jnp.float32), (carry_decay, fresh), unroll=True
     )
     reach = jnp.exp(cumul) * (ids == prev_ids[:, None]).astype(jnp.float32)[:, None, :]
     outside = (
@@ -108,25 +108,12 @@
 
 
 def fetch_weights(w_z, w_x, w_dt, w_bc, w_out, layer_index):
-    owned = (
-        lax.all_gather(w_z[layer_index], "dp", axis=0, tiled=True),
-        lax.all_gather(w_x[layer_index], "dp", axis=0, tiled=True),
-        lax.all_gather(w_dt[layer_index], "dp", axis=0, tiled=True),
-        lax.all_gather(w_out[layer_index], "dp", axis=1, tiled=True),
-    )
-    shared = lax.all_gather(w_bc[layer_index], ("dp", "tensor"), axis=0, tiled=True)
-    return (owned[0], owned[1], owned[2], shared, owned[3])
-
-
-def fetch_again(w_z, w_x, w_dt, w_bc, w_out, layer_index):
-    owned = (
-        lax.all_gather(w_z[layer_index], "dp", axis=0, tiled=True),
-        lax.all_gather(w_x[layer_index], "dp", axis=0, tiled=True),
-        lax.all_gather(w_dt[layer_index], "dp", axis=0, tiled=True),
-        lax.all_gather(w_out[layer_index], "dp", axis=1, tiled=True),
-    )
-    shared = lax.all_gather(w_bc[layer_index], ("dp", "tensor"), axis=0, tiled=True)
-    return (owned[0], owned[1], owned[2], shared, owned[3])
+    shared = lax.all_gather(w_bc[layer_index], "tensor", axis=0, tiled=True)
+    packed = jnp.concatenate(
+        [w_z[layer_index], w_x[layer_index], w_out[layer_index].T, shared, w_dt[layer_index]],
+        axis=1,
+    )
+    return lax.all_gather(packed, "dp", axis=0, tiled=True)
 
 
 def per_device(
@@ -156,18 +143,24 @@
     inner_part = w_z.shape[2]
     head_part = w_dt.shape[2]
     stream = hidden_in.astype(jnp.float32)
+    bc_part = w_bc.shape[2]
+    out_stop = 3 * inner_part
+    bc_stop = out_stop + bc_part
     stored = []
     for layer_index in range(LAYERS):
         weight_set = fetch_weights(w_z, w_x, w_dt, w_bc, w_out, layer_index)
         scale_pre = lax.rsqrt(jnp.mean(stream * stream, axis=1) + epsilon)
         normed = (stream * scale_pre[:, None] * pre_gain[layer_index][None, :]).astype(jnp.bfloat16)
         normed_all = lax.all_gather(normed, "tensor", axis=0, tiled=True)
-        joined = jnp.concatenate(weight_set[:4], axis=1)
-        projected = jnp.dot(normed_all, joined, preferred_element_type=jnp.float32)
+        main_matrix = weight_set[:, : 2 * inner_part]
+        side_matrix = weight_set[:, out_stop:]
+        out_matrix = weight_set[:, 2 * inner_part : out_stop]
+        projected = jnp.dot(normed_all, main_matrix, preferred_element_type=jnp.float32)
+        side = jnp.dot(normed_all, side_matrix, preferred_element_type=jnp.float32)
         gate_raw = projected[:, :inner_part]
-        proj_x = projected[:, inner_part : 2 * inner_part]
-        proj_dt = projected[:, 2 * inner_part : 2 * inner_part + head_part]
-        proj_bc = projected[:, 2 * inner_part + head_part :]
+        proj_x = projected[:, inner_part:]
+        proj_bc = side[:, :bc_part]
+        proj_dt = side[:, bc_part:]
         mixed, back_fn = jax.vjp(
             partial(mixer_core, seg_ids=seg_ids, block_len=SPAN),
             proj_x,
@@ -187,12 +180,11 @@
         normed_out = (gated * scale_gate[:, None] * gate_gain[layer_index][None, :]).astype(
             jnp.bfloat16
         )
-        out_matrix = weight_set[4]
         branch = (
             lax.psum_scatter(
-                jnp.dot(normed_out, out_matrix, preferred_element_type=jnp.float32).astype(
-                    jnp.bfloat16
-                ),
+                jnp.einsum(
+                    "gi,di->gd", normed_out, out_matrix, preferred_element_type=jnp.float32
+                ).astype(jnp.bfloat16),
                 "tensor",
                 scatter_dimension=0,
                 tiled=True,
@@ -210,12 +202,13 @@
                 scale_gate,
                 normed_out,
                 back_fn,
-                weight_set,
+                (main_matrix, side_matrix, out_matrix),
             )
         )
         stream = stream + branch
     hidden_out = stream.astype(jnp.bfloat16)
     grads = [[None] * LAYERS for name_index in range(14)]
+    small = []
     stream_grad = cotangent.astype(jnp.float32)
     for layer_index in reversed(range(LAYERS)):
         (
@@ -230,13 +223,12 @@
             back_fn,
             weight_set,
         ) = stored[layer_index]
-        used_set = fetch_again(w_z, w_x, w_dt, w_bc, w_out, layer_index)
-        joined = jnp.concatenate(used_set[:4], axis=1)
+        main_matrix, side_matrix, out_matrix = weight_set
         branch_grad = (stream_grad * live_rows[:, None]).astype(jnp.bfloat16)
         grad_all = lax.all_gather(branch_grad, "tensor", axis=0, tiled=True)
-        grad_out = jnp.einsum("gi,gd->id", normed_out, grad_all, preferred_element_type=jnp.float32)
+        grad_out = jnp.einsum("gd,gi->di", grad_all, normed_out, preferred_element_type=jnp.float32)
         d_normed_out = jnp.einsum(
-            "gd,id->gi", grad_all, used_set[4], preferred_element_type=jnp.float32
+            "gd,di->gi", grad_all, out_matrix, preferred_element_type=jnp.float32
         )
         gain_row = gate_gain[layer_index]
         grad_gain = jnp.sum(d_normed_out * gated * scale_gate[:, None], axis=0)
@@ -249,41 +241,36 @@
         d_mixed = d_gated * gate_raw * sigmoid_gate
         d_gate_raw = d_gated * mixed * sigmoid_gate * (1.0 + gate_raw * (1.0 - sigmoid_gate))
         pieces = back_fn(d_mixed)
-        d_proj = jnp.concatenate([d_gate_raw, pieces[0], pieces[2], pieces[1]], axis=1).astype(
-            jnp.bfloat16
-        )
-        grad_joined = jnp.einsum(
-            "gd,gk->dk", normed_all, d_proj, preferred_element_type=jnp.float32
-        )
-        grad_wz = grad_joined[:, :inner_part]
-        grad_wx = grad_joined[:, inner_part : 2 * inner_part]
-        grad_wdt = grad_joined[:, 2 * inner_part : 2 * inner_part + head_part]
-        grad_wbc = grad_joined[:, 2 * inner_part + head_part :]
-        owned_grads = (
-            lax.psum_scatter(
-                grad_wz.astype(jnp.bfloat16), "dp", scatter_dimension=0, tiled=True
-            ).astype(jnp.float32),
-            lax.psum_scatter(
-                grad_wx.astype(jnp.bfloat16), "dp", scatter_dimension=0, tiled=True
-            ).astype(jnp.float32),
-            lax.psum_scatter(
-                grad_wdt.astype(jnp.bfloat16), "dp", scatter_dimension=0, tiled=True
-            ).astype(jnp.float32),
-            lax.psum_scatter(
-                grad_out.astype(jnp.bfloat16), "dp", scatter_dimension=1, tiled=True
-            ).astype(jnp.float32),
-        )
+        d_main = jnp.concatenate([d_gate_raw, pieces[0]], axis=1).astype(jnp.bfloat16)
+        d_side = jnp.concatenate([pieces[1], pieces[2]], axis=1).astype(jnp.bfloat16)
+        out_owned = lax.psum_scatter(
+            grad_out.astype(jnp.bfloat16), "dp", scatter_dimension=0, tiled=True
+        )
+        grad_main = jnp.einsum("gd,gk->dk", normed_all, d_main, preferred_element_type=jnp.float32)
+        grad_side = jnp.einsum("gd,gk->dk", normed_all, d_side, preferred_element_type=jnp.float32)
+        owned = lax.psum_scatter(
+            jnp.concatenate(
+                [grad_main.astype(jnp.bfloat16), grad_side.astype(jnp.bfloat16)], axis=1
+            ),
+            "dp",
+            scatter_dimension=0,
+            tiled=True,
+        ).astype(jnp.float32)
+        grads[0][layer_index] = owned[:, :inner_part]
+        grads[1][layer_index] = owned[:, inner_part : 2 * inner_part]
+        grads[2][layer_index] = owned[:, 2 * inner_part + bc_part :]
         grads[3][layer_index] = lax.psum_scatter(
-            grad_wbc, ("dp", "tensor"), scatter_dimension=0, tiled=True
-        )
-        grads[0][layer_index] = owned_grads[0]
-        grads[1][layer_index] = owned_grads[1]
-        grads[2][layer_index] = owned_grads[2]
-        grads[4][layer_index] = owned_grads[3]
+            owned[:, 2 * inner_part : 2 * inner_part + bc_part],
+            "tensor",
+            scatter_dimension=0,
+            tiled=True,
+        )
+        grads[4][layer_index] = out_owned.T.astype(jnp.float32)
         d_normed = lax.psum_scatter(
-            jnp.einsum("gk,dk->gd", d_proj, joined, preferred_element_type=jnp.float32).astype(
-                jnp.bfloat16
-            ),
+            (
+                jnp.einsum("gk,dk->gd", d_main, main_matrix, preferred_element_type=jnp.float32)
+                + jnp.einsum("gk,dk->gd", d_side, side_matrix, preferred_element_type=jnp.float32)
+            ).astype(jnp.bfloat16),
             "tensor",
             scatter_dimension=0,
             tiled=True,
@@ -296,19 +283,27 @@
             + scale_pre[:, None] * pre_row[None, :] * d_normed
             - stream_in * (scale_pre**3 * pre_dot)[:, None]
         )
-        head_sums = lax.psum(
-            (pieces[3], pieces[4], pieces[7], pieces[8], pieces[9], grad_gain), "dp"
-        )
-        shared_sums = lax.psum((pieces[5], pieces[6], grad_pre), ("dp", "tensor"))
-        grads[5][layer_index] = head_sums[0]
-        grads[7][layer_index] = head_sums[1]
-        grads[9][layer_index] = head_sums[2]
-        grads[10][layer_index] = head_sums[3]
-        grads[11][layer_index] = head_sums[4]
-        grads[12][layer_index] = head_sums[5]
-        grads[6][layer_index] = shared_sums[0]
-        grads[8][layer_index] = shared_sums[1]
-        grads[13][layer_index] = shared_sums[2]
+        for place, value in (
+            (6, pieces[5]),
+            (8, pieces[6]),
+            (13, grad_pre),
+            (5, pieces[3]),
+            (7, pieces[4]),
+            (9, pieces[7]),
+            (10, pieces[8]),
+            (11, pieces[9]),
+            (12, grad_gain),
+        ):
+            small.append((place, layer_index, value))
+    small.sort(key=lambda entry: entry[0] not in (6, 8, 13))
+    flat = lax.psum(jnp.concatenate([entry[2].reshape(-1) for entry in small]), "dp")
+    shared_size = sum(entry[2].size for entry in small if entry[0] in (6, 8, 13))
+    shared_flat = lax.psum(flat[:shared_size], "tensor")
+    offset = 0
+    for place, layer_index, value in small:
+        source = shared_flat if place in (6, 8, 13) else flat
+        grads[place][layer_index] = source[offset : offset + value.size].reshape(value.shape)
+        offset += value.size
     stacked = [jnp.stack(entry, axis=0) for entry in grads]
     return (
         hidden_out,

time: 1660 us -> 1420 us (0.86)
  blocking collectives: 304 us -> 47.3 us
  matrix products: 320 us -> 228 us
  waiting for transfers between devices: 578 us -> 649 us
  local copies, waits for them, and re-layouts: 185 us -> 208 us
  other arithmetic: 241 us -> 259 us
    unnamed x32 -> x17, waiting for transfers between devices: 333 us -> 0.28 us
    all_gather x4 -> x2, blocking collectives: 187 us -> 9.86 us  [fetch_weights(): shared = lax.all_gather(w_bc[layer_index], 'tensor', axis=0, tiled=True)]
    reduce_scatter x6 -> x10, waiting for transfers between devices: 217 us -> 349 us  [the longest x2 124 us: per_device(): lax.psum_scatter(grad_out.astype(jnp.bfloat16), 'dp', scatter_dimension=0...]
    all_gather x6 -> x2, waiting for transfers between devices: 0.04 us -> 130 us  [fetch_weights(): return lax.all_gather(packed, 'dp', axis=0, tiled=True)]
    psum x2 -> x1, blocking collectives: 97.9 us -> 8.24 us  [per_device(): shared_flat = lax.psum(flat[:shared_size], 'tensor')]
    psum x0 -> x1, waiting for transfers between devices: none -> 86.5 us  [per_device(): lax.psum(jnp.concatenate([entry[2].reshape(-1) for entry in small]), 'dp')]
    dot_general x6, matrix products: 125 us -> 73.9 us  [state_scan(): inside = jnp.einsum('chij,cjhp->cihp', mixing, xs, precision=highest)]
    all_gather x2, waiting for transfers between devices: 23.8 us -> 51.8 us  [per_device(): normed_all = lax.all_gather(normed, 'tensor', axis=0, tiled=True)]
  transfers between devices with their start and end apart: 24 -> 17, of which waited for: 13 -> 15; matrix products, arithmetic and copies ran while one was open for 31% -> 14% of each run, Pallas kernels for 0% -> 0%
where the time goes in v1:
time: 1420 us; the launch traced here: 1410 us
  waiting for transfers between devices  649 us (46%)
  other arithmetic  259 us (18%)
  matrix products  228 us (16%)
  local copies, waits for them, and re-layouts  208 us (15%)
  blocking collectives  47.3 us (3%)
  between operations  18.1 us (1%)
    all_gather x2, waiting for transfers between devices, fetch_weights(): return lax.all_gather(packed, 'dp', axis=0, tiled=True)  130 us
    reduce_scatter x2, waiting for transfers between devices, per_device(): lax.psum_scatter(grad_out.astype(jnp.bfloat16), 'dp', scatter_dimension=0...  124 us
    reduce_scatter x2, waiting for transfers between devices, per_device(): lax.psum_scatter(jnp.concatenate([grad_main.astype(jnp.bfloat16), grad_si...  118 us
    psum x1, waiting for transfers between devices, per_device(): lax.psum(jnp.concatenate([entry[2].reshape(-1) for entry in small]), 'dp')  86.5 us
    dot_general x6, matrix products, state_scan(): inside = jnp.einsum('chij,cjhp->cihp', mixing, xs, precision=highest)  73.9 us
    reduce_scatter x2, waiting for transfers between devices, per_device(): lax.psum_scatter(jnp.einsum('gi,di->gd', normed_out, out_matrix, preferre...  56.5 us
    unnamed x605, local copies, waits for them, and re-layouts  51.9 us
    all_gather x2, waiting for transfers between devices, per_device(): normed_all = lax.all_gather(normed, 'tensor', axis=0, tiled=True)  51.8 us
  transfers between devices with their start and end apart: 17, of which 15 were waited for; matrix products, arithmetic and copies ran while one was open for 14% of the time, Pallas kernels for 0%

profile of v1, /device:TPU:0, one launch (start us, length us, event | category | flops | bytes accessed | tf_op | source)
XLA Modules:
  0.0 1410.4 jit_solution(14958566650819958388)
XLA Ops:
  29.9 18.5 %all-gather.9.cloned.1.call-done = bf16[1024,1024]{1,0:T(8,128)(2,1)} async-done(((bf16[512,1024]{1,0:T(8,128)(2,1)}), bf16[1024,1024]{1,0:T(8,128)(2,1)}) %all-gather.9.cloned.1.call-update) | async-done | bytes 2097168 | tf_op jit(solution)/shard_map/all_gather | solution.py:154
  48.4 68.9 %all-gather.11.cloned.1.call-done = bf16[1024,3344]{1,0:T(8,128)(2,1)} async-done(((bf16[64,3344]{1,0:T(8,128)(2,1)}), bf16[1024,3344]{1,0:T(8,128)(2,1)}) %all-gather.11.cloned.1.call-update) | async-done | bytes 6848528 | tf_op jit(solution)/shard_map/all_gather | solution.py:116
  151.4 10.0 fusion.41
  179.2 10.4 bitcast_add_fusion.3
  189.6 7.1 copy.769
  196.7 7.6 reshape.885
  204.3 7.1 multiply_reduce_fusion.23
  211.5 14.3 %psum.42 = f32[1024]{0:T(1024)S(1)} all-reduce(f32[1024]{0:T(1024)S(1)} %get-tuple-element.182), channel_id=1, replica_groups=mesh['dp'=16,'tensor'=2] {'tensor'}, use_global_device_ids=true, to_apply=%region_5.7 | all-reduce | flops 1024 | bytes 8192 | tf_op jit(solution)/shard_map/psum | solution.py:178
  238.7 24.7 %reduce-scatter.11.cloned.1.call-done = bf16[512,1024]{1,0:T(8,128)(2,1)} async-done(((bf16[1024,1024]{1,0:T(8,128)(2,1)}), bf16[512,1024]{1,0:T(8,128)(2,1)}) %reduce-scatter.11.cloned.1.call-update) | async-done | bytes 1048592 | tf_op jit(solution)/shard_map/reduce_scatter | solution.py:184
  270.2 61.4 %all-gather.15.cloned.1.call-done = bf16[1024,3344]{1,0:T(8,128)(2,1)} async-done(((bf16[64,3344]{1,0:T(8,128)(2,1)}), bf16[1024,3344]{1,0:T(8,128)(2,1)}) %all-gather.15.cloned.1.call-update) | async-done | bytes 6848528 | tf_op jit(solution)/shard_map/all_gather | solution.py:116
  331.6 33.3 %all-gather.13.cloned.1.call-done = bf16[1024,1024]{1,0:T(8,128)(2,1)} async-done(((bf16[512,1024]{1,0:T(8,128)(2,1)}), bf16[1024,1024]{1,0:T(8,128)(2,1)}) %all-gather.13.cloned.1.call-update) | async-done | bytes 2097168 | tf_op jit(solution)/shard_map/all_gather | solution.py:154
  402.5 9.8 fusion.28
  430.1 10.3 bitcast_add_fusion.2
  440.5 7.2 copy.775
  447.7 7.6 reshape.886
  455.2 7.2 multiply_reduce_fusion.22
  470.6 8.6 multiply_reduce_fusion.12
  484.3 11.4 multiply_reduce_fusion.13
  517.6 17.3 %fusion.13 = (f32[8,16,128]{2,1,0:T(8,128)S(1)}, f32[8,16,128]{2,1,0:T(8,128)S(1)}, f32[8,16,128]{2,1,0:T(8,128)S(1)}, f32[8,128,128]{2,1,0:T(8,128)S(1)}) fusion(f32[8,16,128]{2,1,0:T(8,128)} %copy-done.144, f32[8,16,128]{2,1,0:T(8,128)S(1)} %reduce_window_sum.42, f32[8,128,128]{2,1,0:T(8,128)} %copy-done.117, pred[8,128,128]{2,1,0:T(8,128)(4,1)} %compare_and_fusion, ...), kind=kOutput, calls=%fused_computation.21 | convolution fusion | flops 832389120 | bytes 9895936 | tf_op jit(solution)/shard_map/transpose(jvp(chij,cjhp->cihp))/dot_general | solution.py:53
  574.4 9.4 bitcast_add_fusion.1
  594.7 9.9 reduce_window_sum.43
  616.5 7.2 copy.780
  623.7 7.6 reshape.887
  631.3 8.1 multiply_reduce_fusion.17
  656.9 7.1 fusion.64
  668.2 32.0 %reduce-scatter.15.cloned.1.call-done = bf16[512,1024]{1,0:T(8,128)(2,1)} async-done(((bf16[1024,1024]{1,0:T(8,128)(2,1)}), bf16[512,1024]{1,0:T(8,128)(2,1)}) %reduce-scatter.15.cloned.1.call-update) | async-done | bytes 1048592 | tf_op jit(solution)/shard_map/reduce_scatter | solution.py:269
  708.7 31.0 %all-gather.19.cloned.1.call-done = bf16[1024,1024]{1,0:T(8,128)(2,1)} async-done(((bf16[512,1024]{1,0:T(8,128)(2,1)}), bf16[1024,1024]{1,0:T(8,128)(2,1)}) %all-gather.19.cloned.1.call-update) | async-done | bytes 2097168 | tf_op jit(solution)/shard_map/all_gather | solution.py:228
  739.7 8.6 multiply_reduce_fusion.6
  753.2 11.8 multiply_reduce_fusion.7
  786.3 17.0 %fusion.15 = (f32[8,16,128]{2,1,0:T(8,128)}, f32[8,16,128]{2,1,0:T(8,128)}, f32[8,16,128]{2,1,0:T(8,128)S(1)}, f32[8,128,128]{2,1,0:T(8,128)S(1)}) fusion(f32[8,16,128]{2,1,0:T(8,128)S(1)} %copy-done.142, f32[8,16,128]{2,1,0:T(8,128)S(1)} %copy-done.111, f32[8,128,128]{2,1,0:T(8,128)S(1)} %copy-done.115, pred[8,128,128]{2,1,0:T(8,128)(4,1)S(1)} %copy-done.130, ...), kind=kOutput, calls=%fused_computation.23 | convolution fusion | flops 832389120 | bytes 9895936 | tf_op jit(solution)/shard_map/transpose(jvp(chij,cjhp->cihp))/dot_general | solution.py:53
  837.8 9.5 bitcast_add_fusion
  857.2 9.9 reduce_window_sum.44
  879.1 7.1 copy.787
  886.2 7.6 reshape.888
  893.9 7.6 multiply_reduce_fusion.11
  919.3 7.1 fusion.68
  933.1 7.4 convolution_convert_fusion
  944.0 6.8 convolution_convert_fusion.2
  950.9 6.8 convolution_convert_fusion.3
  971.6 9.8 convolution_convert_fusion.1
  989.6 53.5 %reduce-scatter.21.cloned.1.call-done = bf16[64,2320]{1,0:T(8,128)(2,1)} async-done(((bf16[1024,2320]{1,0:T(8,128)(2,1)}), bf16[64,2320]{1,0:T(8,128)(2,1)}) %reduce-scatter.21.cloned.1.call-update) | async-done | bytes 296976 | tf_op jit(solution)/shard_map/reduce_scatter | solution.py:251
  1048.3 59.6 %reduce-scatter.29.cloned.1.call-done = bf16[64,1024]{1,0:T(8,128)(2,1)} async-done(((bf16[1024,1024]{1,0:T(8,128)(2,1)}), bf16[64,1024]{1,0:T(8,128)(2,1)}) %reduce-scatter.29.cloned.1.call-update) | async-done | bytes 131088 | tf_op jit(solution)/shard_map/reduce_scatter | solution.py:246
  1107.8 64.4 %reduce-scatter.27.cloned.1.call-done = bf16[64,1024]{1,0:T(8,128)(2,1)} async-done(((bf16[1024,1024]{1,0:T(8,128)(2,1)}), bf16[64,1024]{1,0:T(8,128)(2,1)}) %reduce-scatter.27.cloned.1.call-update) | async-done | bytes 131088 | tf_op jit(solution)/shard_map/reduce_scatter | solution.py:246
  1174.0 31.9 %reduce-scatter.13.cloned.1.call-done = bf16[512,1024]{1,0:T(8,128)(2,1)} async-done(((bf16[1024,1024]{1,0:T(8,128)(2,1)}), bf16[512,1024]{1,0:T(8,128)(2,1)}) %reduce-scatter.13.cloned.1.call-update) | async-done | bytes 1048592 | tf_op jit(solution)/shard_map/reduce_scatter | solution.py:184
  1210.0 86.5 %all-reduce.52.cloned.1.call-done = f32[16992]{0:T(1024)} async-done(((f32[16992]{0:T(1024)}), f32[16992]{0:T(1024)}) %all-reduce.52.cloned.1.call-update) | async-done | bytes 67984 | tf_op jit(solution)/shard_map/psum | solution.py:299
  1297.3 8.2 psum.47
  1313.5 64.7 %reduce-scatter.19.cloned.1.call-done = bf16[64,2320]{1,0:T(8,128)(2,1)} async-done(((bf16[1024,2320]{1,0:T(8,128)(2,1)}), bf16[64,2320]{1,0:T(8,128)(2,1)}) %reduce-scatter.19.cloned.1.call-update) | async-done | bytes 296976 | tf_op jit(solution)/shard_map/reduce_scatter | solution.py:251
  1390.0 12.1 reduce-scatter.23.cloned.1.call-done
  (921 shorter events, 439.5 us)
Async XLA Ops:
  7.3 41.1 %all-gather.9.cloned.1.call-start = ((), (), s32[]{:S(2)}) async-start(), calls=%async_computation.10 | async-start | bytes 3145728 | tf_op jit(solution)/shard_map/all_gather | solution.py:154
  9.9 110.1 %copy-start.137 = (f32[1,1024]{1,0:T(1,128)}, f32[1,1024]{1,0:T(1,128)S(1)}, u32[]{:S(2)}) copy-start(f32[1,1024]{1,0:T(1,128)S(1)} %get-tuple-element.268) | copy-start | bytes 12292
  9.9 255.3 %copy-start.131 = (f32[1,1024]{1,0:T(1,128)}, f32[1,1024]{1,0:T(1,128)S(1)}, u32[]{:S(2)}) copy-start(f32[1,1024]{1,0:T(1,128)S(1)} %get-tuple-element.269) | copy-start | bytes 12292
  12.4 104.9 %all-gather.11.cloned.1.call-start = ((), (), s32[]{:S(2)}) async-start(), calls=%async_computation.11 | async-start | bytes 7520256 | tf_op jit(solution)/shard_map/all_gather | solution.py:116
  20.8 242.6 %reduce-scatter.11.cloned.1.call-start = ((), (), s32[]{:S(2)}) async-start(), calls=%async_computation.12 | async-start | bytes 3145728 | tf_op jit(solution)/shard_map/reduce_scatter | solution.py:184
  23.0 98.2 %copy-start.139 = (f32[8,128]{1,0:T(8,128)}, f32[8,128]{1,0:T(8,128)S(1)}, u32[]{:S(2)}) copy-start(f32[8,128]{1,0:T(8,128)S(1)} %get-tuple-element.288) | copy-start | bytes 12292
  23.0 117.6 %copy-start.203 = (pred[8,128]{1,0:T(8,128)(4,1)}, pred[8,128]{1,0:T(8,128)(4,1)S(1)}, u32[]{:S(2)}) copy-start(pred[8,128]{1,0:T(8,128)(4,1)S(1)} %get-tuple-element.289) | copy-start | bytes 3076
  23.2 116.5 %copy-start.229 = (f32[8]{0:T(128)}, f32[8]{0:T(128)S(1)}, u32[]{:S(2)}) copy-start(f32[8]{0:T(128)S(1)} %convert_reduce_fusion.1) | copy-start | bytes 100
  24.7 111.2 %copy-start.254 = (f32[16]{0:T(128)}, f32[16]{0:T(128)S(1)}, u32[]{:S(2)}) copy-start(f32[16]{0:T(128)S(1)} %get-tuple-element.307) | copy-start | bytes 196
  25.3 111.6 %copy-start.256 = (f32[16]{0:T(128)}, f32[16]{0:T(128)S(1)}, u32[]{:S(2)}) copy-start(f32[16]{0:T(128)S(1)} %get-tuple-element.305) | copy-start | bytes 196
  232.5 99.0 %all-gather.15.cloned.1.call-start = ((), (), s32[]{:S(2)}) async-start(), calls=%async_computation.14 | async-start | bytes 7520256 | tf_op jit(solution)/shard_map/all_gather | solution.py:116
  238.5 126.3 %all-gather.13.cloned.1.call-start = ((), (), s32[]{:S(2)}) async-start(), calls=%async_computation.13 | async-start | bytes 3145728 | tf_op jit(solution)/shard_map/all_gather | solution.py:154
  265.2 102.2 %copy-start.151 = (f32[512]{0:T(512)}, f32[512]{0:T(512)S(1)}, u32[]{:S(2)}) copy-start(f32[512]{0:T(512)S(1)} %add_rsqrt_fusion.2) | copy-start | bytes 6148
  268.3 99.1 %copy-start.258 = (f32[16]{0:T(128)S(1)}, f32[16]{0:T(128)}, u32[]{:S(2)}) copy-start(f32[16]{0:T(128)} %get-tuple-element.306) | copy-start | bytes 196
  268.3 99.5 %copy-start.260 = (f32[16]{0:T(128)S(1)}, f32[16]{0:T(128)}, u32[]{:S(2)}) copy-start(f32[16]{0:T(128)} %get-tuple-element.304) | copy-start | bytes 196
  268.4 202.3 %all-gather.17.cloned.1.call-start = ((), (), s32[]{:S(2)}) async-start(), calls=%async_computation.16 | async-start | bytes 3145728 | tf_op jit(solution)/shard_map/all_gather | solution.py:228
  269.3 215.0 %copy-start.149 = (f32[1024]{0:T(1024)}, f32[1024]{0:T(1024)S(1)}, u32[]{:S(2)}) copy-start(f32[1024]{0:T(1024)S(1)} %mul.1818) | copy-start | bytes 12292
  270.1 100.5 %copy-start.230 = (f32[8]{0:T(128)S(1)}, f32[8]{0:T(128)}, u32[]{:S(2)}) copy-start(f32[8]{0:T(128)} %copy-done.229) | copy-start | bytes 100
  270.2 430.0 %reduce-scatter.15.cloned.1.call-start = ((), (), s32[]{:S(2)}) async-start(), calls=%async_computation.17 | async-start | bytes 3145728 | tf_op jit(solution)/shard_map/reduce_scatter | solution.py:269
  367.8 221.9 %copy-start.43 = (f32[8,128,16]{2,0,1:T(8,128)}, f32[8,128,16]{2,0,1:T(8,128)S(1)}, u32[]{:S(2)}) copy-start(f32[8,128,16]{2,0,1:T(8,128)S(1)} %copy.648) | copy-start | bytes 196612
  388.7 39.4 %copy-start.144 = (f32[8,16,128]{2,1,0:T(8,128)}, f32[8,16,128]{2,1,0:T(8,128)S(1)}, u32[]{:S(2)}) copy-start(f32[8,16,128]{2,1,0:T(8,128)S(1)} %copy.650) | copy-start | bytes 196612
  609.9 54.1 %copy-start.123 = (bf16[1024,16]{0,1:T(8,128)(2,1)}, bf16[1024,16]{0,1:T(8,128)(2,1)S(1)}, u32[]{:S(2)}) copy-start(bf16[1024,16]{0,1:T(8,128)(2,1)S(1)} %get-tuple-element.126) | copy-start | bytes 98308
  668.1 38.4 %copy-start.177 = (f32[16]{0:T(128)S(1)}, f32[16]{0:T(128)}, u32[]{:S(2)}) copy-start(f32[16]{0:T(128)} %get-tuple-element.275) | copy-start | bytes 196
  668.1 38.4 %copy-start.181 = (f32[16]{0:T(128)S(1)}, f32[16]{0:T(128)}, u32[]{:S(2)}) copy-start(f32[16]{0:T(128)} %get-tuple-element.274) | copy-start | bytes 196
  668.1 38.4 %copy-start.183 = (f32[16]{0:T(128)S(1)}, f32[16]{0:T(128)}, u32[]{:S(2)}) copy-start(f32[16]{0:T(128)} %get-tuple-element.276) | copy-start | bytes 196
  668.1 38.4 %copy-start.185 = (f32[16]{0:T(128)S(1)}, f32[16]{0:T(128)}, u32[]{:S(2)}) copy-start(f32[16]{0:T(128)} %get-tuple-element.277) | copy-start | bytes 196
  668.1 38.4 %copy-start.234 = (f32[16]{0:T(128)S(1)}, f32[16]{0:T(128)}, u32[]{:S(2)}) copy-start(f32[16]{0:T(128)} %get-tuple-element.278) | copy-start | bytes 196
  668.1 38.4 %copy-start.236 = (f32[16]{0:T(128)S(1)}, f32[16]{0:T(128)}, u32[]{:S(2)}) copy-start(f32[16]{0:T(128)} %get-tuple-element.279) | copy-start | bytes 196
  668.1 71.6 %all-gather.19.cloned.1.call-start = ((), (), s32[]{:S(2)}) async-start(), calls=%async_computation.18 | async-start | bytes 3145728 | tf_op jit(solution)/shard_map/all_gather | solution.py:228
  706.4 274.9 %reduce-scatter.17.cloned.1.call-start = ((), (), s32[]{:S(2)}) async-start(), calls=%async_computation.19 | async-start | bytes 3145728 | tf_op jit(solution)/shard_map/reduce_scatter | solution.py:269
  708.7 44.5 %copy-start.171 = (f32[1024]{0:T(1024)S(1)}, f32[1024]{0:T(1024)}, u32[]{:S(2)}) copy-start(f32[1024]{0:T(1024)} %copy-done.170) | copy-start | bytes 12292
  708.7 44.5 %copy-start.147 = (f32[1024]{0:T(1024)S(1)}, f32[1024]{0:T(1024)}, u32[]{:S(2)}) copy-start(f32[1024]{0:T(1024)} %mul.1732) | copy-start | bytes 12292
  872.5 53.9 %copy-start.125 = (bf16[1024,16]{0,1:T(8,128)(2,1)}, bf16[1024,16]{0,1:T(8,128)(2,1)S(1)}, u32[]{:S(2)}) copy-start(bf16[1024,16]{0,1:T(8,128)(2,1)S(1)} %get-tuple-element.115) | copy-start | bytes 98308
  930.4 112.7 %reduce-scatter.21.cloned.1.call-start = ((), (), s32[]{:S(2)}) async-start(), calls=%async_computation.21 | async-start | bytes 5292032 | tf_op jit(solution)/shard_map/reduce_scatter | solution.py:251
  943.4 164.4 %reduce-scatter.29.cloned.1.call-start = ((), (), s32[]{:S(2)}) async-start(), calls=%async_computation.25 | async-start | bytes 2228224 | tf_op jit(solution)/shard_map/reduce_scatter | solution.py:246
  950.8 221.3 %reduce-scatter.27.cloned.1.call-start = ((), (), s32[]{:S(2)}) async-start(), calls=%async_computation.24 | async-start | bytes 2228224 | tf_op jit(solution)/shard_map/reduce_scatter | solution.py:246
  957.9 247.9 %reduce-scatter.13.cloned.1.call-start = ((), (), s32[]{:S(2)}) async-start(), calls=%async_computation.15 | async-start | bytes 3145728 | tf_op jit(solution)/shard_map/reduce_scatter | solution.py:184
  964.6 332.0 %all-reduce.52.cloned.1.call-start = ((), (), s32[]{:S(2)}) async-start(), calls=%async_computation.26 | async-start | bytes 139264 | tf_op jit(solution)/shard_map/psum | solution.py:299
  984.4 393.8 %reduce-scatter.19.cloned.1.call-start = ((), (), s32[]{:S(2)}) async-start(), calls=%async_computation.20 | async-start | bytes 5292032 | tf_op jit(solution)/shard_map/reduce_scatter | solution.py:251
  989.5 184.5 %copy-start.193 = (f32[512]{0:T(512)S(1)}, f32[512]{0:T(512)}, u32[]{:S(2)}) copy-start(f32[512]{0:T(512)} %copy-done.192) | copy-start | bytes 6148
  989.5 216.3 %copy-start.24 = (bf16[512,1024]{1,0:T(8,128)(2,1)S(1)}, bf16[512,1024]{1,0:T(8,128)(2,1)}, u32[]{:S(2)}) copy-start(bf16[512,1024]{1,0:T(8,128)(2,1)} %reduce-scatter.11.cloned.1.call-done) | copy-start | bytes 3145732
  989.5 216.3 %copy-start.55 = (bf16[512,1024]{1,0:T(8,128)(2,1)S(1)}, bf16[512,1024]{1,0:T(8,128)(2,1)}, u32[]{:S(2)}) copy-start(bf16[512,1024]{1,0:T(8,128)(2,1)} %param.34) | copy-start | bytes 3145732
  989.5 216.3 %copy-start.133 = (f32[1,1024]{1,0:T(1,128)S(1)}, f32[1,1024]{1,0:T(1,128)}, u32[]{:S(2)}) copy-start(f32[1,1024]{1,0:T(1,128)} %copy-done.131) | copy-start | bytes 12292
  989.5 216.3 %copy-start.136 = (f32[512]{0:T(512)S(1)}, f32[512]{0:T(512)}, u32[]{:S(2)}) copy-start(f32[512]{0:T(512)} %copy-done.134) | copy-start | bytes 6148
  989.5 216.3 %copy-start.153 = (f32[512]{0:T(512)S(1)}, f32[512]{0:T(512)}, u32[]{:S(2)}) copy-start(f32[512]{0:T(512)} %copy-done.151) | copy-start | bytes 6148
  989.6 216.3 %copy-start.197 = (f32[512]{0:T(512)S(1)}, f32[512]{0:T(512)}, u32[]{:S(2)}) copy-start(f32[512]{0:T(512)} %copy-done.196) | copy-start | bytes 6148
  989.6 400.4 %reduce-scatter.25.cloned.1.call-start = ((), (), s32[]{:S(2)}) async-start(), calls=%async_computation.23 | async-start | bytes 98304 | tf_op jit(solution)/shard_map/reduce_scatter | solution.py:262
  1048.2 353.8 %reduce-scatter.23.cloned.1.call-start = ((), (), s32[]{:S(2)}) async-start(), calls=%async_computation.22 | async-start | bytes 98304 | tf_op jit(solution)/shard_map/reduce_scatter | solution.py:262
  (256 other events, 2314.1 us)
Sparse Core Ops, SparseCore 0:
  12.5 35.8 all-gather.8
  51.2 66.0 all-gather.10
  232.7 30.6 reduce-scatter.10
  265.5 66.0 all-gather.14
  333.0 31.8 all-gather.12
  366.8 33.0 all-gather.16
  668.2 31.9 reduce-scatter.14
  706.6 33.0 all-gather.18
  930.5 31.8 reduce-scatter.16
  966.2 76.8 reduce-scatter.20
  1046.8 60.9 reduce-scatter.28
  1111.4 60.7 reduce-scatter.26
  1175.0 30.8 reduce-scatter.12
  1209.7 86.7 all-reduce.51
  1300.3 77.7 reduce-scatter.18
  1380.8 9.1 reduce-scatter.24
  1392.0 9.9 reduce-scatter.22
